TPU v7x, 32 devices: a whole 2x2x4 slice. The times are simulated.
32 devices in a mesh: dp: 4 (over z), row: 4 (over y, x), col: 2 (over core).
Axes of the slice: x: 2, y: 2, z: 4, core: 2. Of those that a mesh axis runs over, the one named last changes fastest.
Arguments:
- tokens: bfloat16 [8, 2048, 768], P(('dp', 'col'), 'row'), may hold values from -6 to 6
- cotangent: bfloat16 [8, 2048, 768], P(('dp', 'col'), 'row'), may hold values from -6 to 6
- timesteps: int32 [8], P(('dp', 'col')), may hold values from 0 to 999
- prefix_len: int32 [8], P(('dp', 'col')), may hold values from 204 to 1024, as said below
- time_table: bfloat16 [1000, 768], P('col'), may hold values from -3 to 3
- ln1_gain: float32 [768], replicated, may hold values from 0.25 to 1.75
- ln1_bias: float32 [768], replicated, may hold values from -3 to 3
- w_qkv: bfloat16 [768, 3, 768], P('col', None, 'row'), may hold values from -0.3125 to 0.3125
- w_out: bfloat16 [768, 768], P('col', 'row'), may hold values from -1.75 to 1.75
- out_bias: float32 [768], replicated, may hold values from -3 to 3
- ln2_gain: float32 [768], replicated, may hold values from 0.25 to 1.75
- ln2_bias: float32 [768], replicated, may hold values from -3 to 3
- w_up: bfloat16 [768, 3072], P('col', 'row'), may hold values from -0.21875 to 0.21875
- up_bias: float32 [3072], P('row'), may hold values from -3 to 3
- w_down: bfloat16 [768, 3072], P('col', 'row'), may hold values from -0.109375 to 0.109375
- down_bias: float32 [768], replicated, may hold values from -4 to 4
Outputs:
- layer_out: bfloat16 [8, 2048, 768], P(('dp', 'col'), 'row')
- tokens_grad: float32 [8, 2048, 768], P(('dp', 'col'), 'row')
- table_grad: float32 [1000, 768], P('col')
- ln1_gain_grad: float32 [768], replicated
- ln1_bias_grad: float32 [768], replicated
- qkv_grad: float32 [768, 3, 768], P('col', None, 'row')
- out_grad: float32 [768, 768], P('col', 'row')
- out_bias_grad: float32 [768], replicated
- ln2_gain_grad: float32 [768], replicated
- ln2_bias_grad: float32 [768], replicated
- up_grad: float32 [768, 3072], P('col', 'row')
- up_bias_grad: float32 [3072], P('row')
- down_grad: float32 [768, 3072], P('col', 'row')
- down_bias_grad: float32 [768], replicated
Inputs may be any that keep to these rules, and one draw needn't show every extreme that they name: `prefix_len`: each sequence's prefix length lies between 204 and 1024, and some sequence takes each end.
All inputs are finite; a program needn't handle non-finite values.
Results may differ from a plain program's by a relative error of at most 0.02.
Values may be sent and summed in bfloat16 or wider, within the bound.
A program may use at most 128 MiB of HBM per device.

v0:
```python
import jax
import jax.numpy as jnp
from jax import lax
from jax.sharding import PartitionSpec as P

HD = 64
norm_eps = 1e-05
masked_score = -1e30


def gelu_exact(values):
    return jax.nn.gelu(values, approximate=False)


def gather_rows(values):
    return lax.all_gather(values, "row", axis=1, tiled=True)


def scatter_rows(values):
    return lax.psum_scatter(
        values.astype(jnp.bfloat16), "row", scatter_dimension=1, tiled=True
    ).astype(jnp.float32)


def gather_grads(values):
    return lax.all_gather(values, "row", axis=1, tiled=True)


def scatter_grads(values):
    return lax.psum_scatter(
        values.astype(jnp.bfloat16), "row", scatter_dimension=1, tiled=True
    ).astype(jnp.float32)


def norm_forward(hidden, gain_vec, bias_vec):
    width = hidden.shape[-1]
    average = jnp.sum(hidden, axis=-1, keepdims=True) / width
    variance = jnp.sum(hidden * hidden, axis=-1, keepdims=True) / width - average * average
    inverse = lax.rsqrt(variance + norm_eps)
    centred = (hidden - average) * inverse
    return (centred * gain_vec + bias_vec, centred, inverse)


def norm_backward(grad_out, centred, inverse, gain_vec):
    width = grad_out.shape[-1]
    scaled = grad_out * gain_vec
    first_mean = jnp.sum(scaled, axis=-1, keepdims=True) / width
    second_mean = jnp.sum(scaled * centred, axis=-1, keepdims=True) / width
    grad_in = inverse * (scaled - first_mean - centred * second_mean)
    return (grad_in, jnp.sum(grad_out * centred, axis=(0, 1)), jnp.sum(grad_out, axis=(0, 1)))


def attend_forward(queries, key_rows, values, prefix):
    length = queries.shape[0]
    block_rows = min(512, length)
    score_scale = queries.shape[2] ** (-0.5)
    key_pos = jnp.arange(length, dtype=jnp.int32)

    def one_block(block_index):
        row_start = block_index * block_rows
        query_blk = lax.dynamic_slice_in_dim(queries, row_start, block_rows, 0)
        scores = (
            jnp.einsum("qhd,khd->hqk", query_blk, key_rows, preferred_element_type=jnp.float32)
            * score_scale
        )
        query_pos = row_start + jnp.arange(block_rows, dtype=jnp.int32)
        allowed = (key_pos[None, :] <= query_pos[:, None]) | (key_pos[None, :] < prefix)
        scores = jnp.where(allowed[None], scores, masked_score)
        row_max = jnp.max(scores, axis=2, keepdims=True)
        exponent = jnp.exp(scores - row_max)
        row_total = jnp.sum(exponent, axis=2, keepdims=True)
        soft_low = (exponent / row_total).astype(jnp.bfloat16)
        mixed_blk = jnp.einsum("hqk,khd->qhd", soft_low, values, preferred_element_type=jnp.float32)
        return (mixed_blk, (row_max + jnp.log(row_total))[:, :, 0])

    mixed, logsums = lax.map(one_block, jnp.arange(length // block_rows, dtype=jnp.int32))
    return (mixed.reshape(queries.shape), logsums)


def attend_backward(queries, key_rows, values, mixed, logsums, grad_mixed, prefix):
    length = queries.shape[0]
    block_rows = min(512, length)
    score_scale = queries.shape[2] ** (-0.5)
    key_pos = jnp.arange(length, dtype=jnp.int32)
    delta = jnp.sum(grad_mixed.astype(jnp.float32) * mixed, axis=2)

    def one_block(grads_carry, block_index):
        grad_keys, grad_values = grads_carry
        row_start = block_index * block_rows
        query_blk = lax.dynamic_slice_in_dim(queries, row_start, block_rows, 0)
        grad_blk = lax.dynamic_slice_in_dim(grad_mixed, row_start, block_rows, 0)
        delta_blk = lax.dynamic_slice_in_dim(delta, row_start, block_rows, 0)
        scores = (
            jnp.einsum("qhd,khd->hqk", query_blk, key_rows, preferred_element_type=jnp.float32)
            * score_scale
        )
        query_pos = row_start + jnp.arange(block_rows, dtype=jnp.int32)
        allowed = (key_pos[None, :] <= query_pos[:, None]) | (key_pos[None, :] < prefix)
        scores = jnp.where(allowed[None], scores, masked_score)
        weights_soft = jnp.exp(scores - logsums[block_index][:, :, None])
        grad_soft = jnp.einsum("qhd,khd->hqk", grad_blk, values, preferred_element_type=jnp.float32)
        grad_scores = (weights_soft * (grad_soft - delta_blk.T[:, :, None])).astype(jnp.bfloat16)
        grad_query = (
            jnp.einsum("hqk,khd->qhd", grad_scores, key_rows, preferred_element_type=jnp.float32)
            * score_scale
        )
        grad_keys = (
            grad_keys
            + jnp.einsum("hqk,qhd->khd", grad_scores, query_blk, preferred_element_type=jnp.float32)
            * score_scale
        )
        grad_values = grad_values + jnp.einsum(
            "hqk,qhd->khd",
            weights_soft.astype(jnp.bfloat16),
            grad_blk,
            preferred_element_type=jnp.float32,
        )
        return ((grad_keys, grad_values), grad_query)

    zero_grads = jnp.zeros(key_rows.shape, jnp.float32)
    final_grads, grad_queries = lax.scan(
        one_block, (zero_grads, zero_grads), jnp.arange(length // block_rows, dtype=jnp.int32)
    )
    return jnp.stack([grad_queries.reshape(key_rows.shape), final_grads[0], final_grads[1]], axis=1)


def body(
    tokens,
    cotangent,
    timesteps,
    prefix_len,
    time_table,
    ln1_gain,
    ln1_bias,
    w_qkv,
    w_out,
    out_bias,
    ln2_gain,
    ln2_bias,
    w_up,
    up_bias,
    w_down,
    down_bias,
):
    highest = lax.Precision.HIGHEST
    qkv_full, out_full, up_full, down_full, table_full = (
        lax.all_gather(w_qkv, "col", axis=0, tiled=True),
        lax.all_gather(w_out, "col", axis=0, tiled=True),
        lax.all_gather(w_up, "col", axis=0, tiled=True),
        lax.all_gather(w_down, "col", axis=0, tiled=True),
        lax.all_gather(time_table, "col", axis=0, tiled=True),
    )
    seq_count = tokens.shape[0]
    width_heads = qkv_full.shape[2]
    heads_local = width_heads // HD
    picked = (
        timesteps[:, None] == jnp.arange(table_full.shape[0], dtype=jnp.int32)[None, :]
    ).astype(jnp.float32)
    embed_rows = jnp.dot(picked, table_full.astype(jnp.float32), precision=highest)

    def sequence_forward(seq_item):
        parts_seq, prefix = seq_item
        return attend_forward(parts_seq[:, 0], parts_seq[:, 1], parts_seq[:, 2], prefix)

    def forward_pass(tokens_in):
        hidden0 = tokens_in.astype(jnp.float32) + embed_rows[:, None, :]
        normed1, centred1, inverse1 = norm_forward(hidden0, ln1_gain, ln1_bias)
        full_one = gather_rows(normed1.astype(jnp.bfloat16))
        length = full_one.shape[1]
        project = jnp.einsum(
            "std,dkh->stkh", full_one, qkv_full, preferred_element_type=jnp.float32
        ).astype(jnp.bfloat16)
        parts = project.reshape(seq_count, length, 3, heads_local, HD)
        mixed, logsums = lax.map(sequence_forward, (parts, prefix_len))
        weighted = mixed.reshape(seq_count, length, width_heads).astype(jnp.bfloat16)
        branch = scatter_rows(
            jnp.einsum("sth,dh->std", weighted, out_full, preferred_element_type=jnp.float32)
        )
        hidden1 = hidden0 + (branch + out_bias)
        normed2, centred2, inverse2 = norm_forward(hidden1, ln2_gain, ln2_bias)
        full_two = gather_rows(normed2.astype(jnp.bfloat16))
        inner = (
            jnp.einsum("std,df->stf", full_two, up_full, preferred_element_type=jnp.float32)
            + up_bias
        )
        active = gelu_exact(inner).astype(jnp.bfloat16)
        result = hidden1 + (
            scatter_rows(
                jnp.einsum("stf,df->std", active, down_full, preferred_element_type=jnp.float32)
            )
            + down_bias
        )
        saved = (
            full_one,
            centred1,
            inverse1,
            parts,
            mixed,
            logsums,
            weighted,
            centred2,
            inverse2,
            full_two,
            inner,
            active,
        )
        return (result, saved)

    result, saved = forward_pass(tokens)
    (
        full_one,
        centred1,
        inverse1,
        parts,
        mixed,
        logsums,
        weighted,
        centred2,
        inverse2,
        full_two,
        inner,
        active,
    ) = saved
    length = full_one.shape[1]
    grad_full = gather_grads(cotangent)
    down_grad_full = jnp.einsum(
        "std,stf->df", grad_full, active, preferred_element_type=jnp.float32
    )
    grad_active = jnp.einsum(
        "std,df->stf", grad_full, down_full, preferred_element_type=jnp.float32
    )
    unused_out, gelu_back = jax.vjp(gelu_exact, inner)
    grad_inner = gelu_back(grad_active)[0]
    inner_low = grad_inner.astype(jnp.bfloat16)
    up_grad_full = jnp.einsum(
        "std,stf->df", full_two, inner_low, preferred_element_type=jnp.float32
    )
    grad_normed2 = scatter_grads(
        jnp.einsum("stf,df->std", inner_low, up_full, preferred_element_type=jnp.float32)
    )
    grad_norm_two, ln2_gain_part, ln2_bias_part = norm_backward(
        grad_normed2, centred2, inverse2, ln2_gain
    )
    grad_hidden1 = cotangent.astype(jnp.float32) + grad_norm_two
    grad_branch_full = gather_grads(grad_hidden1.astype(jnp.bfloat16))
    out_grad_full = jnp.einsum(
        "std,sth->dh", grad_branch_full, weighted, preferred_element_type=jnp.float32
    )
    grad_weighted = jnp.einsum(
        "std,dh->sth", grad_branch_full, out_full, preferred_element_type=jnp.float32
    ).astype(jnp.bfloat16)

    def sequence_backward(seq_item):
        parts_seq, mixed_seq, logsum_seq, grad_seq, prefix = seq_item
        return attend_backward(
            parts_seq[:, 0],
            parts_seq[:, 1],
            parts_seq[:, 2],
            mixed_seq,
            logsum_seq,
            grad_seq,
            prefix,
        )

    grad_parts = lax.map(
        sequence_backward,
        (
            parts,
            mixed,
            logsums,
            grad_weighted.reshape(seq_count, length, heads_local, HD),
            prefix_len,
        ),
    )
    grad_project = grad_parts.reshape(seq_count, length, 3, width_heads).astype(jnp.bfloat16)
    qkv_grad_full = jnp.einsum(
        "std,stkh->dkh", full_one, grad_project, preferred_element_type=jnp.float32
    )
    grad_normed1 = scatter_grads(
        jnp.einsum("stkh,dkh->std", grad_project, qkv_full, preferred_element_type=jnp.float32)
    )
    grad_norm_one, ln1_gain_part, ln1_bias_part = norm_backward(
        grad_normed1, centred1, inverse1, ln1_gain
    )
    grad_hidden0 = grad_hidden1 + grad_norm_one
    seq_sums = jnp.sum(grad_hidden0, axis=1)
    table_grad_full = jnp.einsum("sn,sd->nd", picked, seq_sums, precision=highest)
    vectors = lax.psum(
        (
            ln1_gain_part,
            ln1_bias_part,
            jnp.sum(grad_hidden1, axis=(0, 1)),
            ln2_gain_part,
            ln2_bias_part,
            jnp.sum(cotangent.astype(jnp.float32), axis=(0, 1)),
        ),
        ("dp", "row", "col"),
    )
    up_bias_grad = lax.psum(jnp.sum(grad_inner, axis=(0, 1)), ("dp", "col"))
    weights_full = (qkv_grad_full, out_grad_full, up_grad_full, down_grad_full)
    blocks = (
        lax.psum_scatter(
            weights_full[0].astype(jnp.bfloat16), "col", scatter_dimension=0, tiled=True
        ).astype(jnp.float32),
        lax.psum_scatter(
            weights_full[1].astype(jnp.bfloat16), "col", scatter_dimension=0, tiled=True
        ).astype(jnp.float32),
        lax.psum_scatter(
            weights_full[2].astype(jnp.bfloat16), "col", scatter_dimension=0, tiled=True
        ).astype(jnp.float32),
        lax.psum_scatter(
            weights_full[3].astype(jnp.bfloat16), "col", scatter_dimension=0, tiled=True
        ).astype(jnp.float32),
        lax.psum_scatter(
            table_grad_full.astype(jnp.bfloat16), "col", scatter_dimension=0, tiled=True
        ).astype(jnp.float32),
    )
    weight_blocks = (blocks[0], blocks[1], blocks[2], blocks[3])
    weight_blocks = (
        lax.psum(blocks[0].astype(jnp.bfloat16), "dp").astype(jnp.float32),
        lax.psum(blocks[1].astype(jnp.bfloat16), "dp").astype(jnp.float32),
        lax.psum(blocks[2].astype(jnp.bfloat16), "dp").astype(jnp.float32),
        lax.psum(blocks[3].astype(jnp.bfloat16), "dp").astype(jnp.float32),
    )
    table_block = lax.psum(blocks[4].astype(jnp.bfloat16), ("dp", "row")).astype(jnp.float32)
    return (
        result.astype(jnp.bfloat16),
        grad_hidden0,
        table_block,
        vectors[0],
        vectors[1],
        weight_blocks[0],
        weight_blocks[1],
        vectors[2],
        vectors[3],
        vectors[4],
        weight_blocks[2],
        up_bias_grad,
        weight_blocks[3],
        vectors[5],
    )


def solution(mesh):
    placed = (
        P(("dp", "col"), "row", None),
        P(("dp", "col"), "row", None),
        P(("dp", "col")),
        P(("dp", "col")),
        P("col", None),
        P(),
        P(),
        P("col", None, "row"),
        P("col", "row"),
        P(),
        P(),
        P(),
        P("col", "row"),
        P("row"),
        P("col", "row"),
        P(),
    )
    return jax.shard_map(
        body,
        mesh=mesh,
        in_specs=placed,
        out_specs=(
            P(("dp", "col"), "row", None),
            P(("dp", "col"), "row", None),
            P("col", None),
            P(),
            P(),
            P("col", None, "row"),
            P("col", "row"),
            P(),
            P(),
            P(),
            P("col", "row"),
            P("row"),
            P("col", "row"),
            P(),
        ),
        check_vma=False,
    )
```

profile of v0, /device:TPU:0, one launch (start us, length us, event | category | flops | bytes accessed | tf_op | source)
XLA Modules:
  0.0 882.5 jit_solution(11795420427352458064)
XLA Ops:
  8.7 13.4 %all-gather.21.cloned.1.call-done = bf16[2,500,768]{2,1,0:T(8,128)(2,1)} async-done(((bf16[1,500,768]{2,1,0:T(8,128)(2,1)}), bf16[2,500,768]{2,1,0:T(8,128)(2,1)}) %all-gather.21.cloned.1.call-update) | async-done | bytes 1536016 | tf_op jit(solution)/shard_map/all_gather | solution.py:151
  30.4 40.8 %all-gather.9.cloned.1.call-done = bf16[1,2048,768]{2,1,0:T(8,128)(2,1)} async-done(((bf16[1,512,768]{2,1,0:T(8,128)(2,1)}), bf16[1,2048,768]{2,1,0:T(8,128)(2,1)}) %all-gather.9.cloned.1.call-update) | async-done | bytes 3145744 | tf_op jit(solution)/shard_map/all_gather | solution.py:16
  75.7 91.3 %while.50 = (s32[]{:T(128)}, f32[4,512,3,64]{1,3,2,0:T(8,128)}, f32[4,3,512]{2,1,0:T(4,128)S(1)}, s32[4]{0:T(128)S(1)}, s32[]{:T(128)}, /*index=5*/bf16[2048,3,6...) while((s32[]{:T(128)}, f32[4,512,3,64]{1,3,2,0:T(8,128)}, ...), condition=%wide.region_5.6_spmd.clone.clone.clone, body=%wide.region_2.5_spmd.clone.clone.sunk.clone | while | flops 845153280 | bytes 44169396 | solution.py:76
  84.4 6.8 fusion.183
  91.2 7.4 fusion.184
  114.0 7.4 fusion.184
  130.1 6.8 fusion.183
  136.8 7.4 fusion.184
  159.6 7.3 fusion.184
  174.1 43.3 %reduce-scatter.17.cloned.1.call-done = bf16[1,512,768]{2,1,0:T(8,128)(2,1)} async-done(((bf16[1,2048,768]{2,1,0:T(8,128)(2,1)}), bf16[1,512,768]{2,1,0:T(8,128)(2,1)}) %reduce-scatter.17.cloned.1.call-update) | async-done | bytes 786448 | tf_op jit(solution)/shard_map/reduce_scatter | solution.py:20
  228.0 47.4 %all-gather.11.cloned.1.call-done = bf16[1,2048,768]{2,1,0:T(8,128)(2,1)} async-done(((bf16[1,512,768]{2,1,0:T(8,128)(2,1)}), bf16[1,2048,768]{2,1,0:T(8,128)(2,1)}) %all-gather.11.cloned.1.call-update) | async-done | bytes 3145744 | tf_op jit(solution)/shard_map/all_gather | solution.py:16
  275.4 19.0 %multiply_convert_fusion.1 = (bf16[2048,768]{1,0:T(8,128)(2,1)}, f32[2048,768]{1,0:T(8,128)}, f32[2048,768]{1,0:T(8,128)}) fusion(f32[768]{0:T(1024)S(1)} %copy-done.41, bf16[768,768]{1,0:T(8,128)(2,1)} %all-gather.13.cloned.1.call-done, bf16[1,2048,768]{2,1,0:T(8,128)(2,1)} %all-gather.11.cloned.1.call-done), kind=kOutput, calls=%fused_computation.54 | convolution fusion | flops 2519728128 | bytes 20057088 | tf_op jit(solution)/shard_map/std,df->stf/dot_general | solution.py:183
  294.4 38.7 %all-gather.17.cloned.1.call-done = bf16[1,2048,768]{2,1,0:T(8,128)(2,1)} async-done(((bf16[1,512,768]{2,1,0:T(8,128)(2,1)}), bf16[1,2048,768]{2,1,0:T(8,128)(2,1)}) %all-gather.17.cloned.1.call-update) | async-done | bytes 3145744 | tf_op jit(solution)/shard_map/all_gather | solution.py:26
  333.1 11.2 %fusion.112 = (f32[768]{0:T(1024)}, bf16[2048,768]{1,0:T(8,128)(2,1)S(1)}) fusion(f32[2048,768]{1,0:T(8,128)} %get-tuple-element.398, bf16[768,768]{1,0:T(8,128)(2,1)} %all-gather.15.cloned.1.call-done, bf16[1,2048,768]{2,1,0:T(8,128)(2,1)} %all-gather.17.cloned.1.call-done, f32[2048,768]{1,0:T(8,128)} %get-tuple-element.410, f32[768]{0:T(1024)S(1)} %copy-done.41), kind=kOutput, calls=%fused_computation.153 | convolution fusion | flops 2441084160 | bytes 20060160 | tf_op jit(solution)/shard_map/std,df->stf/dot_general | solution.py:229
  356.9 37.2 %reduce-scatter.21.cloned.1.call-done = bf16[1,512,768]{2,1,0:T(8,128)(2,1)} async-done(((bf16[1,2048,768]{2,1,0:T(8,128)(2,1)}), bf16[1,512,768]{2,1,0:T(8,128)(2,1)}) %reduce-scatter.21.cloned.1.call-update) | async-done | bytes 786448 | tf_op jit(solution)/shard_map/reduce_scatter | solution.py:30
  396.8 44.2 %reduce-scatter.19.cloned.1.call-done = bf16[1,512,768]{2,1,0:T(8,128)(2,1)} async-done(((bf16[1,2048,768]{2,1,0:T(8,128)(2,1)}), bf16[1,512,768]{2,1,0:T(8,128)(2,1)}) %reduce-scatter.19.cloned.1.call-update) | async-done | bytes 786448 | tf_op jit(solution)/shard_map/reduce_scatter | solution.py:20
  457.5 34.1 %all-gather.19.cloned.1.call-done = bf16[1,2048,768]{2,1,0:T(8,128)(2,1)} async-done(((bf16[1,512,768]{2,1,0:T(8,128)(2,1)}), bf16[1,2048,768]{2,1,0:T(8,128)(2,1)}) %all-gather.19.cloned.1.call-update) | async-done | bytes 3145744 | tf_op jit(solution)/shard_map/all_gather | solution.py:26
  501.2 87.8 %while.51 = (s32[]{:T(128)}, f32[2048,3,64]{0,2,1:T(8,128)S(1)}, f32[2048,3,64]{0,2,1:T(8,128)}, bf16[4,512,3,64]{1,3,2,0:T(8,128)(2,1)}, s32[4]{0:T(128)S(1)}, ...) while((s32[]{:T(128)}, f32[2048,3,64]{0,2,1:T(8,128)S(1)}, ...), condition=%wide.region_15.16_spmd.clone.clone.clone, body=%wide.region_14.15_spmd.clone.clone.sunk.clone | while | flops 2048887296 | bytes 79087952 | solution.py:121
  618.8 10.4 %reduce-scatter.25.cloned.1.call-done = bf16[384,768]{1,0:T(8,128)(2,1)} async-done(((bf16[768,768]{1,0:T(8,128)(2,1)}), bf16[384,768]{1,0:T(8,128)(2,1)}) %reduce-scatter.25.cloned.1.call-update) | async-done | bytes 589840 | tf_op jit(solution)/shard_map/reduce_scatter | solution.py:308
  629.3 48.0 %reduce-scatter.23.cloned.1.call-done = bf16[1,512,768]{2,1,0:T(8,128)(2,1)} async-done(((bf16[1,2048,768]{2,1,0:T(8,128)(2,1)}), bf16[1,512,768]{2,1,0:T(8,128)(2,1)}) %reduce-scatter.23.cloned.1.call-update) | async-done | bytes 786448 | tf_op jit(solution)/shard_map/reduce_scatter | solution.py:30
  693.0 18.3 %psum.93 = f32[768]{0:T(1024)} all-reduce(f32[768]{0:T(1024)S(1)} %copy-done.37), channel_id=1, replica_groups=mesh['dp'=4,'row'=4,'col'=2] {'dp','col'}, use_global_device_ids=true, to_apply=%region_39.40 | all-reduce | flops 768 | bytes 6144 | tf_op jit(solution)/shard_map/psum | solution.py:299
  711.3 46.5 %all-reduce.9.cloned.1.call-done = (bf16[384,768]{0,1:T(8,128)(2,1)}, bf16[384,3,192]{0,2,1:T(8,128)(2,1)}, bf16[384,192]{0,1:T(8,128)(2,1)}, bf16[384,768]{1,0:T(8,128)(2,1)}) async-done(((bf16[384,768]{0,1:T(8,128)(2,1)}, bf16[384,3,192]{0,2,1:T(8,128)(2,1)}, bf16[384,192]{0,1:T(8,128)(2,1)}, bf16[384,768]{1,0:T(8,128)(2,1)}), (bf16[384,768]{0,1:T(8,128)(2,1)}, bf16[384,3,192]{0,2,1:T(8,128)(2,1)}, ...) | async-done | bytes 1769488 | tf_op jit(solution)/shard_map/psum | solution.py:323
  765.0 40.0 %all-reduce.2 = (f32[768]{0:T(1024)}, f32[768]{0:T(1024)}, f32[768]{0:T(1024)}, f32[768]{0:T(1024)}, f32[768]{0:T(1024)}, /*index=5*/f32[768]{0:T(1024)}) all-reduce(f32[768]{0:T(1024)S(1)} %get-tuple-element.333, f32[768]{0:T(1024)S(1)} %get-tuple-element.342, ...), channel_id=1, replica_groups=mesh['dp'=4,'row'=4,'col'=2] {'dp','row','col'}, use_global_device_ids=true, to_apply=%region_23.24 | all-reduce | flops 4608 | bytes 36864 | tf_op jit(solution)/shard_map/psum | solution.py:288
  804.9 68.4 %all-reduce.7.cloned.1.call-done = bf16[500,768]{1,0:T(8,128)(2,1)} async-done(((bf16[500,768]{1,0:T(8,128)(2,1)}), bf16[500,768]{1,0:T(8,128)(2,1)}) %all-reduce.7.cloned.1.call-update) | async-done | bytes 768016 | tf_op jit(solution)/shard_map/psum | solution.py:325
  (283 shorter events, 248.3 us)
Async XLA Ops:
  7.2 14.9 %all-gather.21.cloned.1.call-start = ((), (), s32[]{:S(2)}) async-start(), calls=%async_computation.20 | async-start | bytes 2322432 | tf_op jit(solution)/shard_map/all_gather | solution.py:151
  7.9 63.2 %all-gather.9.cloned.1.call-start = ((), (), s32[]{:S(2)}) async-start(), calls=%async_computation.8 | async-start | bytes 3932160 | tf_op jit(solution)/shard_map/all_gather | solution.py:16
  24.1 416.9 %copy-start.19 = (f32[768]{0:T(1024)}, f32[768]{0:T(1024)S(1)}, u32[]{:S(2)}) copy-start(f32[768]{0:T(1024)S(1)} %convolution_reduce_fusion) | copy-start | bytes 9220
  25.9 191.5 %reduce-scatter.17.cloned.1.call-start = ((), (), s32[]{:S(2)}) async-start(), calls=%async_computation.9 | async-start | bytes 3932160 | tf_op jit(solution)/shard_map/reduce_scatter | solution.py:20
  173.2 54.8 %all-gather.13.cloned.1.call-start = ((), (), s32[]{:S(2)}) async-start(), calls=%async_computation.11 | async-start | bytes 1769472 | tf_op jit(solution)/shard_map/all_gather | solution.py:149
  173.8 101.6 %copy-start.41 = (f32[768]{0:T(1024)S(1)}, f32[768]{0:T(1024)}, u32[]{:S(2)}) copy-start(f32[768]{0:T(1024)} %param.33) | copy-start | bytes 9220
  173.8 101.6 %all-gather.11.cloned.1.call-start = ((), (), s32[]{:S(2)}) async-start(), calls=%async_computation.10 | async-start | bytes 3932160 | tf_op jit(solution)/shard_map/all_gather | solution.py:16
  221.6 72.8 %all-gather.15.cloned.1.call-start = ((), (), s32[]{:S(2)}) async-start(), calls=%async_computation.12 | async-start | bytes 1769472 | tf_op jit(solution)/shard_map/all_gather | solution.py:150
  222.2 110.9 %all-gather.17.cloned.1.call-start = ((), (), s32[]{:S(2)}) async-start(), calls=%async_computation.14 | async-start | bytes 3932160 | tf_op jit(solution)/shard_map/all_gather | solution.py:26
  222.9 171.2 %reduce-scatter.21.cloned.1.call-start = ((), (), s32[]{:S(2)}) async-start(), calls=%async_computation.15 | async-start | bytes 3932160 | tf_op jit(solution)/shard_map/reduce_scatter | solution.py:30
  350.0 91.1 %reduce-scatter.19.cloned.1.call-start = ((), (), s32[]{:S(2)}) async-start(), calls=%async_computation.13 | async-start | bytes 3932160 | tf_op jit(solution)/shard_map/reduce_scatter | solution.py:20
  356.8 84.2 %copy-start.36 = (f32[768]{0:T(1024)S(1)}, f32[768]{0:T(1024)}, u32[]{:S(2)}) copy-start(f32[768]{0:T(1024)} %param.35) | copy-start | bytes 9220
  356.9 134.8 %all-gather.19.cloned.1.call-start = ((), (), s32[]{:S(2)}) async-start(), calls=%async_computation.16 | async-start | bytes 3932160 | tf_op jit(solution)/shard_map/all_gather | solution.py:26
  447.5 165.3 %reduce-scatter.31.cloned.1.call-start = ((), (), s32[]{:S(2)}) async-start(), calls=%async_computation.23 | async-start | bytes 1769472
  457.5 157.6 %reduce-scatter.29.cloned.1.call-start = ((), (), s32[]{:S(2)}) async-start(), calls=%async_computation.22 | async-start | bytes 589824
  596.3 20.5 %reduce-scatter.27.cloned.1.call-start = ((), (), s32[]{:S(2)}) async-start(), calls=%async_computation.21 | async-start | bytes 1474560
  601.7 27.5 %reduce-scatter.25.cloned.1.call-start = ((), (), s32[]{:S(2)}) async-start(), calls=%async_computation.19 | async-start | bytes 1769472 | tf_op jit(solution)/shard_map/reduce_scatter | solution.py:308
  608.5 68.7 %reduce-scatter.23.cloned.1.call-start = ((), (), s32[]{:S(2)}) async-start(), calls=%async_computation.17 | async-start | bytes 3932160 | tf_op jit(solution)/shard_map/reduce_scatter | solution.py:30
  612.7 145.1 %all-reduce.9.cloned.1.call-start = ((), (), s32[]{:S(2)}) async-start(), calls=%async_computation.24 | async-start | bytes 3538944 | tf_op jit(solution)/shard_map/psum | solution.py:323
  629.3 244.1 %all-reduce.7.cloned.1.call-start = ((), (), s32[]{:S(2)}) async-start(), calls=%async_computation.18 | async-start | bytes 1548288 | tf_op jit(solution)/shard_map/psum | solution.py:325
  686.9 3.5 collective-permute-start
  693.0 72.0 %copy-start.31 = (f32[768]{0:T(1024)S(1)}, f32[768]{0:T(1024)}, u32[]{:S(2)}) copy-start(f32[768]{0:T(1024)} %get-tuple-element.341) | copy-start | bytes 9220
  693.0 72.0 %copy-start.32 = (f32[768]{0:T(1024)S(1)}, f32[768]{0:T(1024)}, u32[]{:S(2)}) copy-start(f32[768]{0:T(1024)} %get-tuple-element.393) | copy-start | bytes 9220
  693.0 72.0 %copy-start.33 = (f32[768]{0:T(1024)S(1)}, f32[768]{0:T(1024)}, u32[]{:S(2)}) copy-start(f32[768]{0:T(1024)} %get-tuple-element.405) | copy-start | bytes 9220
  (46 other events, 987.2 us)
Sparse Core Ops, SparseCore 0:
  9.6 12.4 all-gather.20
  26.0 45.1 all-gather.8
  173.4 43.9 reduce-scatter.16
  218.8 9.1 all-gather.12
  230.3 45.1 all-gather.10
  276.8 9.2 all-gather.14
  287.9 45.1 all-gather.16
  350.1 43.9 reduce-scatter.20
  397.1 43.9 reduce-scatter.18
  447.6 43.9 all-gather.18
  494.4 8.6 reduce-scatter.30
  596.4 7.6 reduce-scatter.28
  606.9 9.6 reduce-scatter.26
  619.4 9.8 reduce-scatter.24
  632.1 45.1 reduce-scatter.22
  680.9 76.8 all-reduce.8
  764.4 108.9 all-reduce.6
where the time goes:
time: 892 us; the launch traced here: 882 us
  waiting for transfers between devices  480 us (54%)
  matrix products  196 us (22%)
  other arithmetic  72.5 us (8%)
  blocking collectives  67.1 us (8%)
  local copies, waits for them, and re-layouts  33.4 us (4%)
  between operations  16.1 us (2%)
  loops' own time  14.2 us (2%)
    all_gather x2, waiting for transfers between devices, gather_rows(): return lax.all_gather(values, 'row', axis=1, tiled=True)  88.2 us
    reduce_scatter x2, waiting for transfers between devices, scatter_rows(): lax.psum_scatter(values.astype(jnp.bfloat16), 'row', scatter_dimension=1,...  87.5 us
    reduce_scatter x2, waiting for transfers between devices, scatter_grads(): lax.psum_scatter(values.astype(jnp.bfloat16), 'row', scatter_dimension=1,...  85.2 us
    all_gather x2, waiting for transfers between devices, gather_grads(): return lax.all_gather(values, 'row', axis=1, tiled=True)  72.8 us
    psum x1, waiting for transfers between devices, body(): lax.psum(blocks[4].astype(jnp.bfloat16), ('dp', 'row')).astype(jnp.float32)  68.4 us
    psum x1, waiting for transfers between devices, body(): lax.psum(blocks[3].astype(jnp.bfloat16), 'dp').astype(jnp.float32)  46.5 us
    psum x1, blocking collectives, body(): lax.psum((ln1_gain_part, ln1_bias_part, jnp.sum(grad_hidden1, axis=(0, 1)...  40 us
    dot_general x8, matrix products, one_block(): jnp.einsum('qhd,khd->hqk', query_blk, key_rows, preferred_element_type=jn...  31.4 us
  transfers between devices with their start and end apart: 18, of which 13 were waited for; matrix products, arithmetic and copies ran while one was open for 20% of the time, Pallas kernels for 0%

commit v1 on v0

--- a/solution.py
+++ b/solution.py
@@ -1,3 +1,4 @@
+import functools
 import jax
 import jax.numpy as jnp
 from jax import lax
@@ -8,12 +9,45 @@
 masked_score = -1e30
 
 
+def routes_all_list(work_x, out_dim):
+    k_now = list(work_x.shape[1:])
+    k_now[out_dim] *= work_x.shape[0]
+    v_now = jnp.moveaxis(work_x, 0, out_dim).reshape(k_now)
+    return v_now
+
+
+def use_sheet(my_tile, along_axis):
+    fan = lax.axis_size(along_axis)
+    state_now = my_tile[None]
+    for dev_j in range(fan.bit_length() - 1):
+        current_arr = 1 << dev_j
+        shaped = lax.ppermute(
+            state_now,
+            axis_name=along_axis,
+            perm=[(to_i, to_i ^ current_arr) for to_i in range(fan)],
+        )
+        ready = jnp.stack([state_now, shaped], 0)
+        latest = lax.axis_index(along_axis)
+        later = latest >> dev_j & 1
+        state_now = jnp.where(later == 0, ready, ready[::-1]).reshape(-1, *my_tile.shape)
+    return state_now
+
+
+def return_all_skins(obj, frame, in_dim):
+    res = use_sheet(obj, frame)
+    then = routes_all_list(res, in_dim)
+    return then
+
+
+supply_all_side_over_axis = functools.partial(return_all_skins, frame="row", in_dim=1)
+
+
 def gelu_exact(values):
     return jax.nn.gelu(values, approximate=False)
 
 
 def gather_rows(values):
-    return lax.all_gather(values, "row", axis=1, tiled=True)
+    return supply_all_side_over_axis(values)
 
 
 def scatter_rows(values):

time: 892 us -> 874 us (0.980)
  waiting for transfers between devices: 480 us -> 456 us
  other arithmetic: 72.5 us -> 82.4 us
    ppermute x0 -> x4, waiting for transfers between devices: none -> 107 us  [use_sheet(): lax.ppermute(state_now, axis_name=along_axis, perm=[(to_i, to_i ^ current...]
    all_gather x2 -> x0, waiting for transfers between devices: 88.2 us -> none  [gather_rows(): return lax.all_gather(values, 'row', axis=1, tiled=True)]
    all_gather x2, waiting for transfers between devices: 72.8 us -> 34.1 us  [gather_grads(): return lax.all_gather(values, 'row', axis=1, tiled=True)]
    another operation x5 -> x13, other arithmetic: 2.06 us -> 11.7 us  [the longest x8 9.66 us: use_sheet(): ready = jnp.stack([state_now, shaped], 0)]
    unnamed x93 -> x95, local copies, waits for them, and re-layouts: 23.4 us -> 23.7 us
  transfers between devices with their start and end apart: 18 -> 20, of which waited for: 13 -> 13; matrix products, arithmetic and copies ran while one was open for 20% -> 21% of each run, Pallas kernels for 0% -> 0%
where the time goes in v1:
time: 874 us; the launch traced here: 870 us
  waiting for transfers between devices  456 us (52%)
  matrix products  191 us (22%)
  other arithmetic  82.4 us (9%)
  blocking collectives  67.7 us (8%)
  local copies, waits for them, and re-layouts  34.6 us (4%)
  between operations  16.1 us (2%)
  loops' own time  12.6 us (1%)
  starting transfers between devices  9.86 us (1%)
    ppermute x4, waiting for transfers between devices, use_sheet(): lax.ppermute(state_now, axis_name=along_axis, perm=[(to_i, to_i ^ current...  107 us
    reduce_scatter x2, waiting for transfers between devices, scatter_rows(): lax.psum_scatter(values.astype(jnp.bfloat16), 'row', scatter_dimension=1,...  89.5 us
    reduce_scatter x2, waiting for transfers between devices, scatter_grads(): lax.psum_scatter(values.astype(jnp.bfloat16), 'row', scatter_dimension=1,...  85.2 us
    psum x1, waiting for transfers between devices, body(): lax.psum(blocks[4].astype(jnp.bfloat16), ('dp', 'row')).astype(jnp.float32)  68.4 us
    psum x1, waiting for transfers between devices, body(): lax.psum(blocks[3].astype(jnp.bfloat16), 'dp').astype(jnp.float32)  46.5 us
    psum x1, blocking collectives, body(): lax.psum((ln1_gain_part, ln1_bias_part, jnp.sum(grad_hidden1, axis=(0, 1)...  40 us
    all_gather x2, waiting for transfers between devices, gather_grads(): return lax.all_gather(values, 'row', axis=1, tiled=True)  34.1 us
    dot_general x8, matrix products, one_block(): jnp.einsum('qhd,khd->hqk', query_blk, key_rows, preferred_element_type=jn...  31.3 us
  transfers between devices with their start and end apart: 20, of which 13 were waited for; matrix products, arithmetic and copies ran while one was open for 21% of the time, Pallas kernels for 0%

profile of v1, /device:TPU:0, one launch (start us, length us, event | category | flops | bytes accessed | tf_op | source)
XLA Modules:
  0.0 869.7 jit_solution(2679915666197426648)
XLA Ops:
  8.7 13.4 %all-gather.15.cloned.1.call-done = bf16[2,500,768]{2,1,0:T(8,128)(2,1)} async-done(((bf16[1,500,768]{2,1,0:T(8,128)(2,1)}), bf16[2,500,768]{2,1,0:T(8,128)(2,1)}) %all-gather.15.cloned.1.call-update) | async-done | bytes 1536016 | tf_op jit(solution)/shard_map/all_gather | solution.py:185
  26.8 18.0 %collective-permute-done = bf16[1,1,512,768]{3,2,1,0:T(8,128)(2,1)S(1)} collective-permute-done((bf16[1,1,512,768]{3,2,1,0:T(8,128)(2,1)S(1)}, bf16[1,1,512,768]{3,2,1,0:T(8,128)(2,1)S(1)}, u32[]{:S(2)}, u32[]{:S(2)}) %collective-permute-start) | collective-permute-done | bytes 786464 | tf_op jit(solution)/shard_map/ppermute | solution.py:24
  53.3 29.3 %collective-permute-done.1 = bf16[2,1,512,768]{3,2,0,1:T(8,128)(2,1)} collective-permute-done((bf16[2,1,512,768]{3,2,0,1:T(8,128)(2,1)}, bf16[2,1,512,768]{3,2,0,1:T(8,128)(2,1)}, u32[]{:S(2)}, u32[]{:S(2)}) %collective-permute-start.1) | collective-permute-done | bytes 1572896 | tf_op jit(solution)/shard_map/ppermute | solution.py:24
  88.3 89.1 %while.50 = (s32[]{:T(128)}, f32[4,512,3,64]{1,3,2,0:T(8,128)S(1)}, f32[4,3,512]{2,1,0:T(4,128)S(1)}, s32[4]{0:T(128)S(1)}, s32[]{:T(128)}, /*index=5*/bf16[2048...) while((s32[]{:T(128)}, f32[4,512,3,64]{1,3,2,0:T(8,128)S(1)}, ...), condition=%wide.region_5.6_spmd.clone.clone.clone, body=%wide.region_2.5_spmd.clone.clone.sunk.clone | while | flops 845153280 | bytes 47319244 | solution.py:110
  97.0 6.8 fusion.188
  119.3 6.8 fusion.188
  126.1 6.8 fusion.189
  141.5 6.8 fusion.188
  163.8 6.8 fusion.188
  182.4 45.2 %reduce-scatter.17.cloned.1.call-done = bf16[1,512,768]{2,1,0:T(8,128)(2,1)} async-done(((bf16[1,2048,768]{2,1,0:T(8,128)(2,1)}), bf16[1,512,768]{2,1,0:T(8,128)(2,1)}) %reduce-scatter.17.cloned.1.call-update) | async-done | bytes 786448 | tf_op jit(solution)/shard_map/reduce_scatter | solution.py:54
  234.2 17.4 %collective-permute-done.2 = bf16[1,1,512,768]{3,2,1,0:T(8,128)(2,1)} collective-permute-done((bf16[1,1,512,768]{3,2,1,0:T(8,128)(2,1)}, bf16[1,1,512,768]{3,2,1,0:T(8,128)(2,1)}, u32[]{:S(2)}, u32[]{:S(2)}) %collective-permute-start.2) | collective-permute-done | bytes 786464 | tf_op jit(solution)/shard_map/ppermute | solution.py:24
  256.9 41.9 %collective-permute-done.3 = bf16[2,1,512,768]{3,2,0,1:T(8,128)(2,1)} collective-permute-done((bf16[2,1,512,768]{3,2,0,1:T(8,128)(2,1)}, bf16[2,1,512,768]{3,2,0,1:T(8,128)(2,1)}, u32[]{:S(2)}, u32[]{:S(2)}) %collective-permute-start.3) | collective-permute-done | bytes 1572896 | tf_op jit(solution)/shard_map/ppermute | solution.py:24
  303.2 19.0 %multiply_convert_fusion.1 = (bf16[2048,768]{1,0:T(8,128)(2,1)}, f32[2048,768]{1,0:T(8,128)}, f32[2048,768]{1,0:T(8,128)}) fusion(f32[768]{0:T(1024)S(1)} %copy-done.43, bf16[2048,768]{1,0:T(8,128)(2,1)} %bitcast.214, bf16[768,768]{1,0:T(8,128)(2,1)} %all-gather.7.cloned.1.call-done), kind=kOutput, calls=%fused_computation.54 | convolution fusion | flops 2519728128 | bytes 20057088 | tf_op jit(solution)/shard_map/std,df->stf/dot_general | solution.py:217
  322.2 11.2 %fusion.109 = (f32[768]{0:T(1024)}, bf16[2048,768]{1,0:T(8,128)(2,1)S(1)}) fusion(f32[2048,768]{1,0:T(8,128)} %get-tuple-element.398, bf16[768,768]{1,0:T(8,128)(2,1)} %all-gather.9.cloned.1.call-done, bf16[1,2048,768]{2,1,0:T(8,128)(2,1)} %all-gather.11.cloned.1.call-done, f32[2048,768]{1,0:T(8,128)} %get-tuple-element.416, f32[768]{0:T(1024)S(1)} %copy-done.43), kind=kOutput, calls=%fused_computation.160 | convolution fusion | flops 2441084160 | bytes 20060160 | tf_op jit(solution)/shard_map/std,df->stf/dot_general | solution.py:263
  346.2 37.1 %reduce-scatter.21.cloned.1.call-done = bf16[1,512,768]{2,1,0:T(8,128)(2,1)} async-done(((bf16[1,2048,768]{2,1,0:T(8,128)(2,1)}), bf16[1,512,768]{2,1,0:T(8,128)(2,1)}) %reduce-scatter.21.cloned.1.call-update) | async-done | bytes 786448 | tf_op jit(solution)/shard_map/reduce_scatter | solution.py:64
  386.0 44.2 %reduce-scatter.19.cloned.1.call-done = bf16[1,512,768]{2,1,0:T(8,128)(2,1)} async-done(((bf16[1,2048,768]{2,1,0:T(8,128)(2,1)}), bf16[1,512,768]{2,1,0:T(8,128)(2,1)}) %reduce-scatter.19.cloned.1.call-update) | async-done | bytes 786448 | tf_op jit(solution)/shard_map/reduce_scatter | solution.py:54
  446.6 34.1 %all-gather.13.cloned.1.call-done = bf16[1,2048,768]{2,1,0:T(8,128)(2,1)} async-done(((bf16[1,512,768]{2,1,0:T(8,128)(2,1)}), bf16[1,2048,768]{2,1,0:T(8,128)(2,1)}) %all-gather.13.cloned.1.call-update) | async-done | bytes 3145744 | tf_op jit(solution)/shard_map/all_gather | solution.py:60
  490.4 85.8 %while.51 = (s32[]{:T(128)}, f32[2048,3,64]{0,2,1:T(8,128)S(1)}, f32[2048,3,64]{0,2,1:T(8,128)}, bf16[4,512,3,64]{1,3,2,0:T(8,128)(2,1)}, s32[4]{0:T(128)S(1)}, ...) while((s32[]{:T(128)}, f32[2048,3,64]{0,2,1:T(8,128)S(1)}, ...), condition=%wide.region_15.16_spmd.clone.clone.clone, body=%wide.region_14.15_spmd.clone.clone.sunk.clone | while | flops 2048887296 | bytes 79087952 | solution.py:155
  605.9 10.4 %reduce-scatter.25.cloned.1.call-done = bf16[384,768]{1,0:T(8,128)(2,1)} async-done(((bf16[768,768]{1,0:T(8,128)(2,1)}), bf16[384,768]{1,0:T(8,128)(2,1)}) %reduce-scatter.25.cloned.1.call-update) | async-done | bytes 589840 | tf_op jit(solution)/shard_map/reduce_scatter | solution.py:342
  616.4 48.1 %reduce-scatter.23.cloned.1.call-done = bf16[1,512,768]{2,1,0:T(8,128)(2,1)} async-done(((bf16[1,2048,768]{2,1,0:T(8,128)(2,1)}), bf16[1,512,768]{2,1,0:T(8,128)(2,1)}) %reduce-scatter.23.cloned.1.call-update) | async-done | bytes 786448 | tf_op jit(solution)/shard_map/reduce_scatter | solution.py:64
  680.2 18.3 %psum.93 = f32[768]{0:T(1024)} all-reduce(f32[768]{0:T(1024)S(1)} %copy-done.40), channel_id=1, replica_groups=mesh['dp'=4,'row'=4,'col'=2] {'dp','col'}, use_global_device_ids=true, to_apply=%region_39.40 | all-reduce | flops 768 | bytes 6144 | tf_op jit(solution)/shard_map/psum | solution.py:333
  698.5 46.5 %all-reduce.9.cloned.1.call-done = (bf16[384,768]{0,1:T(8,128)(2,1)}, bf16[384,3,192]{0,2,1:T(8,128)(2,1)}, bf16[384,192]{0,1:T(8,128)(2,1)}, bf16[384,768]{1,0:T(8,128)(2,1)}) async-done(((bf16[384,768]{0,1:T(8,128)(2,1)}, bf16[384,3,192]{0,2,1:T(8,128)(2,1)}, bf16[384,192]{0,1:T(8,128)(2,1)}, bf16[384,768]{1,0:T(8,128)(2,1)}), (bf16[384,768]{0,1:T(8,128)(2,1)}, bf16[384,3,192]{0,2,1:T(8,128)(2,1)}, ...) | async-done | bytes 1769488 | tf_op jit(solution)/shard_map/psum | solution.py:357
  752.2 40.0 %all-reduce.2 = (f32[768]{0:T(1024)}, f32[768]{0:T(1024)}, f32[768]{0:T(1024)}, f32[768]{0:T(1024)}, f32[768]{0:T(1024)}, /*index=5*/f32[768]{0:T(1024)}) all-reduce(f32[768]{0:T(1024)S(1)} %get-tuple-element.333, f32[768]{0:T(1024)S(1)} %get-tuple-element.342, ...), channel_id=1, replica_groups=mesh['dp'=4,'row'=4,'col'=2] {'dp','row','col'}, use_global_device_ids=true, to_apply=%region_23.24 | all-reduce | flops 4608 | bytes 36864 | tf_op jit(solution)/shard_map/psum | solution.py:322
  792.1 68.4 %all-reduce.7.cloned.1.call-done = bf16[500,768]{1,0:T(8,128)(2,1)} async-done(((bf16[500,768]{1,0:T(8,128)(2,1)}), bf16[500,768]{1,0:T(8,128)(2,1)}) %all-reduce.7.cloned.1.call-update) | async-done | bytes 768016 | tf_op jit(solution)/shard_map/psum | solution.py:359
  (304 shorter events, 264.4 us)
Async XLA Ops:
  7.2 14.9 %all-gather.15.cloned.1.call-start = ((), (), s32[]{:S(2)}) async-start(), calls=%async_computation.18 | async-start | bytes 2322432 | tf_op jit(solution)/shard_map/all_gather | solution.py:185
  7.9 219.7 %reduce-scatter.17.cloned.1.call-start = ((), (), s32[]{:S(2)}) async-start(), calls=%async_computation.8 | async-start | bytes 3932160 | tf_op jit(solution)/shard_map/reduce_scatter | solution.py:54
  25.0 19.8 %collective-permute-start = (bf16[1,1,512,768]{3,2,1,0:T(8,128)(2,1)S(1)}, bf16[1,1,512,768]{3,2,1,0:T(8,128)(2,1)S(1)}, u32[]{:S(2)}, u32[]{:S(2)}) collective-permute-start(bf16[1,1,512,768]{3,2,1,0:T(8,128)(2,1)S(1)} %get-tuple-element.410), channel_id=1, source_target_pairs={{0,2},{2,0},{4,6},{6,4},{1,3},{3,1},{5,7},{7,5},{8,10},{10,8},{12,... | collective-permute-start | bytes 2359304 | tf_op jit(solution)/shard_map/ppermute | solution.py:24
  46.4 36.1 %collective-permute-start.1 = (bf16[2,1,512,768]{3,2,0,1:T(8,128)(2,1)}, bf16[2,1,512,768]{3,2,0,1:T(8,128)(2,1)}, u32[]{:S(2)}, u32[]{:S(2)}) collective-permute-start(bf16[2,1,512,768]{3,2,0,1:T(8,128)(2,1)} %get-tuple-element.408), channel_id=1, source_target_pairs={{0,4},{2,6},{4,0},{6,2},{1,5},{3,7},{5,1},{7,3},{8,12},{10,14},{12... | collective-permute-start | bytes 4718600 | tf_op jit(solution)/shard_map/ppermute | solution.py:24
  182.4 120.9 %all-gather.7.cloned.1.call-start = ((), (), s32[]{:S(2)}) async-start(), calls=%async_computation.9 | async-start | bytes 1769472 | tf_op jit(solution)/shard_map/all_gather | solution.py:183
  231.9 19.6 %collective-permute-start.2 = (bf16[1,1,512,768]{3,2,1,0:T(8,128)(2,1)}, bf16[1,1,512,768]{3,2,1,0:T(8,128)(2,1)}, u32[]{:S(2)}, u32[]{:S(2)}) collective-permute-start(bf16[1,1,512,768]{3,2,1,0:T(8,128)(2,1)} %fusion.141), channel_id=1, source_target_pairs={{0,2},{2,0},{4,6},{6,4},{1,3},{3,1},{5,7},{7,5},{8,10},{10,8},{12,... | collective-permute-start | bytes 2359304 | tf_op jit(solution)/shard_map/ppermute | solution.py:24
  233.4 88.8 %all-gather.9.cloned.1.call-start = ((), (), s32[]{:S(2)}) async-start(), calls=%async_computation.10 | async-start | bytes 1769472 | tf_op jit(solution)/shard_map/all_gather | solution.py:184
  254.8 44.0 %collective-permute-start.3 = (bf16[2,1,512,768]{3,2,0,1:T(8,128)(2,1)}, bf16[2,1,512,768]{3,2,0,1:T(8,128)(2,1)}, u32[]{:S(2)}, u32[]{:S(2)}) collective-permute-start(bf16[2,1,512,768]{3,2,0,1:T(8,128)(2,1)} %get-tuple-element.406), channel_id=1, source_target_pairs={{0,4},{2,6},{4,0},{6,2},{1,5},{3,7},{5,1},{7,3},{8,12},{10,14},{12... | collective-permute-start | bytes 4718600 | tf_op jit(solution)/shard_map/ppermute | solution.py:24
  256.2 66.0 %all-gather.11.cloned.1.call-start = ((), (), s32[]{:S(2)}) async-start(), calls=%async_computation.12 | async-start | bytes 3932160 | tf_op jit(solution)/shard_map/all_gather | solution.py:60
  256.8 126.5 %reduce-scatter.21.cloned.1.call-start = ((), (), s32[]{:S(2)}) async-start(), calls=%async_computation.13 | async-start | bytes 3932160 | tf_op jit(solution)/shard_map/reduce_scatter | solution.py:64
  339.1 91.1 %reduce-scatter.19.cloned.1.call-start = ((), (), s32[]{:S(2)}) async-start(), calls=%async_computation.11 | async-start | bytes 3932160 | tf_op jit(solution)/shard_map/reduce_scatter | solution.py:54
  346.1 84.1 %copy-start.39 = (f32[768]{0:T(1024)S(1)}, f32[768]{0:T(1024)}, u32[]{:S(2)}) copy-start(f32[768]{0:T(1024)} %param.35) | copy-start | bytes 9220
  346.2 134.5 %all-gather.13.cloned.1.call-start = ((), (), s32[]{:S(2)}) async-start(), calls=%async_computation.14 | async-start | bytes 3932160 | tf_op jit(solution)/shard_map/all_gather | solution.py:60
  436.6 163.3 %reduce-scatter.31.cloned.1.call-start = ((), (), s32[]{:S(2)}) async-start(), calls=%async_computation.21 | async-start | bytes 1769472
  446.6 155.6 %reduce-scatter.29.cloned.1.call-start = ((), (), s32[]{:S(2)}) async-start(), calls=%async_computation.20 | async-start | bytes 589824
  583.4 20.5 %reduce-scatter.27.cloned.1.call-start = ((), (), s32[]{:S(2)}) async-start(), calls=%async_computation.19 | async-start | bytes 1474560
  588.8 27.5 %reduce-scatter.25.cloned.1.call-start = ((), (), s32[]{:S(2)}) async-start(), calls=%async_computation.17 | async-start | bytes 1769472 | tf_op jit(solution)/shard_map/reduce_scatter | solution.py:342
  595.6 68.8 %reduce-scatter.23.cloned.1.call-start = ((), (), s32[]{:S(2)}) async-start(), calls=%async_computation.15 | async-start | bytes 3932160 | tf_op jit(solution)/shard_map/reduce_scatter | solution.py:64
  599.8 145.2 %all-reduce.9.cloned.1.call-start = ((), (), s32[]{:S(2)}) async-start(), calls=%async_computation.22 | async-start | bytes 3538944 | tf_op jit(solution)/shard_map/psum | solution.py:357
  616.3 244.2 %all-reduce.7.cloned.1.call-start = ((), (), s32[]{:S(2)}) async-start(), calls=%async_computation.16 | async-start | bytes 1548288 | tf_op jit(solution)/shard_map/psum | solution.py:359
  674.1 3.5 collective-permute-start.4
  680.2 72.0 %copy-start.35 = (f32[768]{0:T(1024)S(1)}, f32[768]{0:T(1024)}, u32[]{:S(2)}) copy-start(f32[768]{0:T(1024)} %get-tuple-element.341) | copy-start | bytes 9220
  680.2 72.0 %copy-start.36 = (f32[768]{0:T(1024)S(1)}, f32[768]{0:T(1024)}, u32[]{:S(2)}) copy-start(f32[768]{0:T(1024)} %get-tuple-element.393) | copy-start | bytes 9220
  680.2 72.0 %copy-start.37 = (f32[768]{0:T(1024)S(1)}, f32[768]{0:T(1024)}, u32[]{:S(2)}) copy-start(f32[768]{0:T(1024)} %get-tuple-element.411) | copy-start | bytes 9220
  (53 other events, 956.6 us)
Sparse Core Ops, SparseCore 0:
  9.6 12.4 all-gather.14
  182.5 45.1 reduce-scatter.16
  233.5 9.2 all-gather.6
  256.3 9.2 all-gather.8
  267.3 53.6 all-gather.10
  339.2 44.0 reduce-scatter.20
  386.3 43.9 reduce-scatter.18
  436.7 43.9 all-gather.12
  483.5 8.6 reduce-scatter.30
  583.5 7.6 reduce-scatter.28
  594.0 9.6 reduce-scatter.26
  606.5 9.8 reduce-scatter.24
  619.3 45.1 reduce-scatter.22
  668.1 76.8 all-reduce.8
  751.6 108.9 all-reduce.6
